TPU v7x, 32 devices: a whole 2x2x4 slice. The times are simulated.
32 devices in a mesh: col: 8 (over z, y), lev: 4 (over x, core).
Axes of the slice: x: 2, y: 2, z: 4, core: 2. Of those that a mesh axis runs over, the one named last changes fastest.
Arguments:
- state_anom: bfloat16 [48, 64, 8192], P('lev', None, 'col'), may hold values from -6 to 6
- error_sum: float32 [48, 8192], P('lev', 'col'), may hold values from -3 to 3
- obs_anom: bfloat16 [64, 16384], P('lev', 'col'), may hold values from -6 to 6
- local_weight: float32 [32, 16384], P(None, 'col'), may hold values from 0.05 to 1
- neighbours: int32 [32, 16384], P(None, 'col'), may hold values from 0 to 3071, as said below
- innovation: float32 [16384], P(('col', 'lev')), may hold values from -6 to 6
- obs_type: int32 [16384], P(('col', 'lev')), may hold values from 0 to 31
- live: int32 [16384], P(('col', 'lev')), may hold values 0 or 1
Outputs:
- impact: float32 [16384], P(('col', 'lev'))
- type_impact: float32 [32], replicated
Inputs may be any that keep to these rules, and one draw needn't show every extreme that they name: Observation o lies in column tile o // 2048; the column (o // 2048 - 1) * 1024 + neighbours[n, o] lies in that tile or the tile on either side of it, inside the grid.
All inputs are finite; a program needn't handle non-finite values. No bound on the sum of `live` on one device may be relied on, other than what follows from the above.
Results may differ from a plain program's by a relative error of at most 0.0003.
Values may be sent and summed in bfloat16 or wider, within the bound.
A program may use at most 64 MiB of HBM per device.

v0:
```python
import math
import jax
import jax.numpy as jnp
from jax import lax
from jax.sharding import PartitionSpec as P

MEMBERS = 64
NTYPE = 32


def with_halo(cells, sides, width):
    for axis, dim in sides:
        count = lax.axis_size(axis)
        ends = count - 1
        head = lax.slice_in_dim(cells, 0, width, axis=dim)
        tail = lax.slice_in_dim(cells, cells.shape[dim] - width, cells.shape[dim], axis=dim)
        cells = jnp.concatenate(
            [
                lax.ppermute(tail, axis, [(i, (i + 1) % count) for i in range(ends)]),
                cells,
                lax.ppermute(head, axis, [((i + 1) % count, i) for i in range(ends)]),
            ],
            axis=dim,
        )
    return cells


def block_pairs(extended, anom, weight, index):
    span = extended.shape[1]
    column_ids = lax.broadcasted_iota(jnp.int32, (span, index.shape[1]), 0)
    table = jnp.sum(
        jnp.where(index[:, None, :] == column_ids[None, :, :], weight[:, None, :], 0.0), axis=0
    )
    spread = jnp.dot(
        extended, table, precision=lax.Precision.HIGHEST, preferred_element_type=jnp.float32
    )
    return jnp.sum(anom.astype(jnp.float32) * spread, axis=0)


def shards(state_anom, error_sum, obs_anom, local_weight, neighbours, innovation, obs_type, live):
    columns = state_anom.shape[2]
    regrouped = lax.all_to_all(state_anom, "lev", split_axis=1, concat_axis=0, tiled=True)
    all_error = lax.all_gather(error_sum, "lev", axis=0, tiled=True)
    sens = jnp.einsum(
        "lkc,lc->kc", regrouped.astype(jnp.float32), all_error, precision=lax.Precision.HIGHEST
    )
    extended = with_halo(sens, (("col", 1),), columns)
    obs_slots = obs_anom.shape[1]
    step_rows = math.gcd(obs_slots, 512)
    count = obs_slots // step_rows
    groups = obs_anom.shape[0]
    anom_blocks = jnp.transpose(obs_anom.reshape(groups, count, step_rows), (1, 0, 2))
    weight_blocks = jnp.transpose(
        local_weight.reshape(local_weight.shape[0], count, step_rows), (1, 0, 2)
    )
    index_blocks = jnp.transpose(
        neighbours.reshape(neighbours.shape[0], count, step_rows), (1, 0, 2)
    )

    def one_block(items):
        return block_pairs(extended, items[0], items[1], items[2])

    partial_pair = lax.map(one_block, (anom_blocks, weight_blocks, index_blocks)).reshape(obs_slots)
    pair = lax.psum_scatter(partial_pair, "lev", scatter_dimension=0, tiled=True)
    impact = pair * innovation * live.astype(jnp.float32) / (MEMBERS - 1.0)
    onehot = (obs_type[None, :] == jnp.arange(NTYPE, dtype=jnp.int32)[:, None]).astype(jnp.float32)
    type_part = jnp.sum(onehot * impact[None, :], axis=1)
    type_impact = lax.psum(type_part, ("col", "lev"))
    return (impact, type_impact)


def solution(mesh):
    in_specs = (
        P("lev", None, "col"),
        P("lev", "col"),
        P("lev", "col"),
        P(None, "col"),
        P(None, "col"),
        P(("col", "lev")),
        P(("col", "lev")),
        P(("col", "lev")),
    )
    out_specs = (P(("col", "lev")), P())
    return jax.shard_map(shards, mesh=mesh, in_specs=in_specs, out_specs=out_specs, check_vma=False)
```

profile of v0, /device:TPU:0, one launch (start us, length us, event | category | flops | bytes accessed | tf_op | source)
XLA Modules:
  0.0 241.2 jit_solution(3400720630463568245)
XLA Ops:
  0.6 0.0 copy-start.2
  0.6 0.0 copy-start
  0.6 3.7 %copy.23 = bf16[12,64,1024]{2,0,1:T(8,128)(2,1)} copy(bf16[12,64,1024]{2,1,0:T(8,128)(2,1)} %param.10) | data formatting | bytes 3145728 | tf_op args[0]
  4.4 4.4 %all-to-all-start = ((bf16[12,64,1024]{2,0,1:T(8,128)(2,1)}), bf16[12,64,1024]{2,0,1:T(8,128)(2,1)S(1)}, u32[]{:S(2)}, u32[]{:S(2)}) async-start(bf16[12,64,1024]{2,0,1:T(8,128)(2,1)} %copy.23), calls=%async_computation | async-start | bytes 4194304 | tf_op jit(solution)/shard_map/all_to_all | solution.py:42
  8.7 0.0 copy-done.2
  8.7 27.9 %all-gather = f32[4,12,1024]{2,1,0:T(8,128)S(1)} all-gather(f32[1,12,1024]{2,1,0:T(8,128)S(1)} %bitcast.60), channel_id=1, replica_groups=mesh['col'=8,'lev'=4] {'lev'}, dimensions={0}, use_global_device_ids=true | all-gather | bytes 245760 | tf_op jit(solution)/shard_map/all_gather | solution.py:43
  36.7 0.0 all-to-all-done
  36.7 0.9 copy.36
  37.6 0.4 multiply_reduce_fusion
  38.0 4.2 %collective-permute-start = (f32[16,1024]{1,0:T(8,128)S(1)}, f32[16,1024]{1,0:T(8,128)S(1)}, u32[]{:S(2)}, u32[]{:S(2)}) collective-permute-start(f32[16,1024]{1,0:T(8,128)S(1)} %bitcast.55), channel_id=1, source_target_pairs={{0,4},{4,8},{8,12},{12,16},{16,20},{20,24},{24,28},{1,5},{5,9},{9,... | collective-permute-start | bytes 196616 | tf_op jit(solution)/shard_map/ppermute | solution.py:19
  42.3 1.3 collective-permute-start.1
  43.6 0.0 copy-done
  43.6 0.2 reshape.25
  43.8 0.0 copy-done.1
  43.8 0.2 reshape.26
  43.9 0.0 copy-done.3
  44.0 0.0 copy-done.8
  44.0 0.6 dynamic-slice
  45.3 0.0 collective-permute-done
  45.3 3.1 %collective-permute-done.1 = f32[16,1024]{1,0:T(8,128)S(1)} collective-permute-done((f32[16,1024]{1,0:T(8,128)S(1)}, f32[16,1024]{1,0:T(8,128)S(1)}, u32[]{:S(2)}, u32[]{:S(2)}) %collective-permute-start.1) | collective-permute-done | bytes 65568 | tf_op jit(solution)/shard_map/ppermute | solution.py:21
  48.4 0.0 copy-start.5
  48.4 0.0 copy-start.6
  48.5 0.0 copy-start.7
  48.5 146.3 %while.10 = (s32[]{:T(128)}, f32[4,512]{1,0:T(4,128)S(1)}, bf16[4,16,512]{2,1,0:T(8,128)(2,1)S(1)}, s32[4,32,512]{2,0,1:T(4,128)S(1)}, f32[4,32,512]{2,0,1:T(4,1...) while((s32[]{:T(128)}, f32[4,512]{1,0:T(4,128)S(1)}, bf16[4,16,512]{2,1,0:T(8,128)(2,1)S(1)}, ...), condition=%wide.region_3.4_spmd, body=%wide.region_0.3_spmd.sunk | while | flops 451436032 | bytes 13457509 | solution.py:63
  48.5 0.1 constant_dynamic-slice_fusion.4
  48.6 0.1 constant_dynamic-slice_fusion.5
  48.6 30.9 %select_reduce_fusion.3 = f32[3072,512]{1,0:T(8,128)} fusion(f32[32,512]{1,0:T(8,128)S(1)} %bitcast.50, s32[32,512]{1,0:T(8,128)S(1)} %bitcast.51), kind=kLoop, calls=%fused_computation.clone.1 | loop fusion | flops 149422080 | bytes 6422528 | tf_op jit(solution)/shard_map/while/body/eval_jaxpr/reduce_sum | solution.py:31
  79.6 5.4 %fusion.11 = f32[512]{0:T(512)S(1)} fusion(f32[3072,512]{1,0:T(8,128)} %select_reduce_fusion.3, f32[16,3072]{1,0:T(8,128)S(1)} %get-tuple-element.129, bf16[4,16,512]{2,1,0:T(8,128)(2,1)S(1)} %get-tuple-element.126, s32[]{:T(128)} %get-tuple-element.116), kind=kOutput, calls=%fused_computation.4.clone.1 | convolution fusion | flops 302013952 | bytes 6506500 | tf_op jit(solution)/shard_map/while/body/eval_jaxpr/dot_general | solution.py:34
  85.0 0.1 dynamic_update_slice.5
  85.0 0.1 constant_dynamic-slice_fusion.4
  85.1 0.1 constant_dynamic-slice_fusion.5
  85.2 30.9 %select_reduce_fusion.3 = f32[3072,512]{1,0:T(8,128)} fusion(f32[32,512]{1,0:T(8,128)S(1)} %bitcast.50, s32[32,512]{1,0:T(8,128)S(1)} %bitcast.51), kind=kLoop, calls=%fused_computation.clone.1 | loop fusion | flops 149422080 | bytes 6422528 | tf_op jit(solution)/shard_map/while/body/eval_jaxpr/reduce_sum | solution.py:31
  116.1 5.4 %fusion.11 = f32[512]{0:T(512)S(1)} fusion(f32[3072,512]{1,0:T(8,128)} %select_reduce_fusion.3, f32[16,3072]{1,0:T(8,128)S(1)} %get-tuple-element.129, bf16[4,16,512]{2,1,0:T(8,128)(2,1)S(1)} %get-tuple-element.126, s32[]{:T(128)} %get-tuple-element.116), kind=kOutput, calls=%fused_computation.4.clone.1 | convolution fusion | flops 302013952 | bytes 6506500 | tf_op jit(solution)/shard_map/while/body/eval_jaxpr/dot_general | solution.py:34
  121.5 0.1 dynamic_update_slice.5
  121.6 0.1 constant_dynamic-slice_fusion.4
  121.7 0.1 constant_dynamic-slice_fusion.5
  121.8 30.9 %select_reduce_fusion.3 = f32[3072,512]{1,0:T(8,128)} fusion(f32[32,512]{1,0:T(8,128)S(1)} %bitcast.50, s32[32,512]{1,0:T(8,128)S(1)} %bitcast.51), kind=kLoop, calls=%fused_computation.clone.1 | loop fusion | flops 149422080 | bytes 6422528 | tf_op jit(solution)/shard_map/while/body/eval_jaxpr/reduce_sum | solution.py:31
  152.7 5.4 %fusion.11 = f32[512]{0:T(512)S(1)} fusion(f32[3072,512]{1,0:T(8,128)} %select_reduce_fusion.3, f32[16,3072]{1,0:T(8,128)S(1)} %get-tuple-element.129, bf16[4,16,512]{2,1,0:T(8,128)(2,1)S(1)} %get-tuple-element.126, s32[]{:T(128)} %get-tuple-element.116), kind=kOutput, calls=%fused_computation.4.clone.1 | convolution fusion | flops 302013952 | bytes 6506500 | tf_op jit(solution)/shard_map/while/body/eval_jaxpr/dot_general | solution.py:34
  158.1 0.1 dynamic_update_slice.5
  158.2 0.1 constant_dynamic-slice_fusion.4
  158.3 0.1 constant_dynamic-slice_fusion.5
  158.4 30.9 %select_reduce_fusion.3 = f32[3072,512]{1,0:T(8,128)} fusion(f32[32,512]{1,0:T(8,128)S(1)} %bitcast.50, s32[32,512]{1,0:T(8,128)S(1)} %bitcast.51), kind=kLoop, calls=%fused_computation.clone.1 | loop fusion | flops 149422080 | bytes 6422528 | tf_op jit(solution)/shard_map/while/body/eval_jaxpr/reduce_sum | solution.py:31
  189.3 5.4 %fusion.11 = f32[512]{0:T(512)S(1)} fusion(f32[3072,512]{1,0:T(8,128)} %select_reduce_fusion.3, f32[16,3072]{1,0:T(8,128)S(1)} %get-tuple-element.129, bf16[4,16,512]{2,1,0:T(8,128)(2,1)S(1)} %get-tuple-element.126, s32[]{:T(128)} %get-tuple-element.116), kind=kOutput, calls=%fused_computation.4.clone.1 | convolution fusion | flops 302013952 | bytes 6506500 | tf_op jit(solution)/shard_map/while/body/eval_jaxpr/dot_general | solution.py:34
  194.7 0.1 dynamic_update_slice.5
  194.8 5.9 %all-reduce = f32[2048]{0:T(1024)S(1)} all-reduce(f32[2048]{0:T(1024)S(1)} %bitcast.61), channel_id=2, replica_groups=mesh['col'=8,'lev'=4] {'lev'}, use_global_device_ids=true, to_apply=%region_4.5.clone | all-reduce | flops 2048 | bytes 16384
  200.7 0.1 fusion.3
  200.8 0.1 select_reduce_fusion.1
  200.9 40.3 %psum.7 = f32[32]{0:T(128)} all-reduce(f32[32]{0:T(128)S(1)} %select_reduce_fusion.1), channel_id=1, replica_groups=mesh['col'=8,'lev'=4] {'col','lev'}, use_global_device_ids=true, to_apply=%region_6.7 | all-reduce | flops 32 | bytes 256 | tf_op jit(solution)/shard_map/psum | solution.py:68
  (22 shorter events, 0.2 us)
Async XLA Ops:
  0.6 8.1 %copy-start.2 = (f32[12,1024]{1,0:T(8,128)S(1)}, f32[12,1024]{1,0:T(8,128)}, u32[]{:S(2)}) copy-start(f32[12,1024]{1,0:T(8,128)} %param.11) | copy-start | bytes 147460
  0.6 42.9 %copy-start = (s32[32,2048]{1,0:T(8,128)S(1)}, s32[32,2048]{1,0:T(8,128)}, u32[]{:S(2)}) copy-start(s32[32,2048]{1,0:T(8,128)} %param.14) | copy-start | bytes 786436
  4.4 39.4 %copy-start.1 = (f32[32,2048]{1,0:T(8,128)S(1)}, f32[32,2048]{1,0:T(8,128)}, u32[]{:S(2)}) copy-start(f32[32,2048]{1,0:T(8,128)} %param.13) | copy-start | bytes 786436
  4.4 39.6 %copy-start.3 = (bf16[16,2048]{1,0:T(8,128)(2,1)S(1)}, bf16[16,2048]{1,0:T(8,128)(2,1)}, u32[]{:S(2)}) copy-start(bf16[16,2048]{1,0:T(8,128)(2,1)} %param.12) | copy-start | bytes 196612
  4.4 39.7 %copy-start.8 = (u32[32]{0:T(128)S(1)}, u32[32]{0:T(128)}, u32[]{:S(2)}) copy-start(u32[32]{0:T(128)} %constant.27) | copy-start | bytes 388
  4.4 32.3 %all-to-all-start = ((bf16[12,64,1024]{2,0,1:T(8,128)(2,1)}), bf16[12,64,1024]{2,0,1:T(8,128)(2,1)S(1)}, u32[]{:S(2)}, u32[]{:S(2)}) async-start(bf16[12,64,1024]{2,0,1:T(8,128)(2,1)} %copy.23), calls=%async_computation | async-start | bytes 4194304 | tf_op jit(solution)/shard_map/all_to_all | solution.py:42
  38.0 7.3 %collective-permute-start = (f32[16,1024]{1,0:T(8,128)S(1)}, f32[16,1024]{1,0:T(8,128)S(1)}, u32[]{:S(2)}, u32[]{:S(2)}) collective-permute-start(f32[16,1024]{1,0:T(8,128)S(1)} %bitcast.55), channel_id=1, source_target_pairs={{0,4},{4,8},{8,12},{12,16},{16,20},{20,24},{24,28},{1,5},{5,9},{9,... | collective-permute-start | bytes 196616 | tf_op jit(solution)/shard_map/ppermute | solution.py:19
  42.3 6.2 %collective-permute-start.1 = (f32[16,1024]{1,0:T(8,128)S(1)}, f32[16,1024]{1,0:T(8,128)S(1)}, u32[]{:S(2)}, u32[]{:S(2)}) collective-permute-start(f32[16,1024]{1,0:T(8,128)S(1)} %bitcast.56), channel_id=1, source_target_pairs={{4,0},{8,4},{12,8},{16,12},{20,16},{24,20},{28,24},{5,1},{9,5},{13... | collective-permute-start | bytes 196616 | tf_op jit(solution)/shard_map/ppermute | solution.py:21
  48.4 152.2 %copy-start.5 = (f32[512]{0:T(512)S(1)}, f32[512]{0:T(512)}, u32[]{:S(2)}) copy-start(f32[512]{0:T(512)} %param.15) | copy-start | bytes 6148
  48.4 152.2 %copy-start.6 = (s32[512]{0:T(512)S(1)}, s32[512]{0:T(512)}, u32[]{:S(2)}) copy-start(s32[512]{0:T(512)} %param.17) | copy-start | bytes 6148
  48.5 152.3 %copy-start.7 = (s32[512]{0:T(512)S(1)}, s32[512]{0:T(512)}, u32[]{:S(2)}) copy-start(s32[512]{0:T(512)} %param.16) | copy-start | bytes 6148
  200.7 40.4 %copy-start.4 = (f32[512]{0:T(512)}, f32[512]{0:T(512)S(1)}, u32[]{:S(2)}) copy-start(f32[512]{0:T(512)S(1)} %fusion.3) | copy-start | bytes 6148
where the time goes:
time: 242 us; the launch traced here: 241 us
  other arithmetic  124 us (51%)
  blocking collectives  74.1 us (31%)
  matrix products  21.7 us (9%)
  starting transfers between devices  9.9 us (4%)
  local copies, waits for them, and re-layouts  6.36 us (3%)
  waiting for transfers between devices  3.13 us (1%)
    reduce_sum x4, other arithmetic, block_pairs(): jnp.sum(jnp.where(index[:, None, :] == column_ids[None, :, :], weight[:,...  124 us
    psum x1, blocking collectives, shards(): type_impact = lax.psum(type_part, ('col', 'lev'))  40.3 us
    all_gather x1, blocking collectives, shards(): all_error = lax.all_gather(error_sum, 'lev', axis=0, tiled=True)  27.9 us
    dot_general x4, matrix products, block_pairs(): jnp.dot(extended, table, precision=lax.Precision.HIGHEST, preferred_eleme...  21.7 us
    unnamed x1, blocking collectives  5.87 us
    unnamed x23, local copies, waits for them, and re-layouts  5.23 us
  transfers between devices with their start and end apart: 3, of which 1 were waited for; matrix products, arithmetic and copies ran while one was open for 0% of the time, Pallas kernels for 0%

commit v1 on v0

--- a/solution.py
+++ b/solution.py
@@ -65,7 +65,7 @@
     impact = pair * innovation * live.astype(jnp.float32) / (MEMBERS - 1.0)
     onehot = (obs_type[None, :] == jnp.arange(NTYPE, dtype=jnp.int32)[:, None]).astype(jnp.float32)
     type_part = jnp.sum(onehot * impact[None, :], axis=1)
-    type_impact = lax.psum(type_part, ("col", "lev"))
+    type_impact = lax.psum(lax.psum(type_part, "lev"), "col")
     return (impact, type_impact)
 
 

time: 242 us -> 227 us (0.938)
  blocking collectives: 74.1 us -> 59.8 us
    psum x1 -> x2, blocking collectives: 40.3 us -> 26.1 us  [shards(): type_impact = lax.psum(lax.psum(type_part, 'lev'), 'col')]
where the time goes in v1:
time: 227 us
  other arithmetic  124 us (55%)
  blocking collectives  59.8 us (26%)
  matrix products  21.7 us (10%)
  starting transfers between devices  9.9 us (4%)
  local copies, waits for them, and re-layouts  6.36 us (3%)
  waiting for transfers between devices  3.13 us (1%)
    reduce_sum x4, other arithmetic, block_pairs(): jnp.sum(jnp.where(index[:, None, :] == column_ids[None, :, :], weight[:,...  124 us
    all_gather x1, blocking collectives, shards(): all_error = lax.all_gather(error_sum, 'lev', axis=0, tiled=True)  27.9 us
    psum x2, blocking collectives, shards(): type_impact = lax.psum(lax.psum(type_part, 'lev'), 'col')  26.1 us
    dot_general x4, matrix products, block_pairs(): jnp.dot(extended, table, precision=lax.Precision.HIGHEST, preferred_eleme...  21.7 us
    unnamed x1, blocking collectives  5.87 us
    unnamed x23, local copies, waits for them, and re-layouts  5.23 us
  transfers between devices with their start and end apart: 3, of which 1 were waited for; matrix products, arithmetic and copies ran while one was open for 0% of the time, Pallas kernels for 0%

profile of v1, /device:TPU:0, one launch (start us, length us, event | category | flops | bytes accessed | tf_op | source)
XLA Modules:
  0.0 226.9 jit_solution(17100901206780303438)
XLA Ops:
  0.6 0.0 copy-start.2
  0.6 0.0 copy-start
  0.6 3.7 %copy.23 = bf16[12,64,1024]{2,0,1:T(8,128)(2,1)} copy(bf16[12,64,1024]{2,1,0:T(8,128)(2,1)} %param.10) | data formatting | bytes 3145728 | tf_op args[0]
  4.4 4.4 %all-to-all-start = ((bf16[12,64,1024]{2,0,1:T(8,128)(2,1)}), bf16[12,64,1024]{2,0,1:T(8,128)(2,1)S(1)}, u32[]{:S(2)}, u32[]{:S(2)}) async-start(bf16[12,64,1024]{2,0,1:T(8,128)(2,1)} %copy.23), calls=%async_computation | async-start | bytes 4194304 | tf_op jit(solution)/shard_map/all_to_all | solution.py:42
  8.7 0.0 copy-done.2
  8.7 27.9 %all-gather = f32[4,12,1024]{2,1,0:T(8,128)S(1)} all-gather(f32[1,12,1024]{2,1,0:T(8,128)S(1)} %bitcast.60), channel_id=1, replica_groups=mesh['col'=8,'lev'=4] {'lev'}, dimensions={0}, use_global_device_ids=true | all-gather | bytes 245760 | tf_op jit(solution)/shard_map/all_gather | solution.py:43
  36.7 0.0 all-to-all-done
  36.7 0.9 copy.36
  37.6 0.4 multiply_reduce_fusion
  38.0 4.2 %collective-permute-start = (f32[16,1024]{1,0:T(8,128)S(1)}, f32[16,1024]{1,0:T(8,128)S(1)}, u32[]{:S(2)}, u32[]{:S(2)}) collective-permute-start(f32[16,1024]{1,0:T(8,128)S(1)} %bitcast.55), channel_id=1, source_target_pairs={{0,4},{4,8},{8,12},{12,16},{16,20},{20,24},{24,28},{1,5},{5,9},{9,... | collective-permute-start | bytes 196616 | tf_op jit(solution)/shard_map/ppermute | solution.py:19
  42.3 1.3 collective-permute-start.1
  43.6 0.0 copy-done
  43.6 0.2 reshape.25
  43.8 0.0 copy-done.1
  43.8 0.2 reshape.26
  43.9 0.0 copy-done.3
  44.0 0.6 dynamic-slice
  45.3 0.0 collective-permute-done
  45.3 3.1 %collective-permute-done.1 = f32[16,1024]{1,0:T(8,128)S(1)} collective-permute-done((f32[16,1024]{1,0:T(8,128)S(1)}, f32[16,1024]{1,0:T(8,128)S(1)}, u32[]{:S(2)}, u32[]{:S(2)}) %collective-permute-start.1) | collective-permute-done | bytes 65568 | tf_op jit(solution)/shard_map/ppermute | solution.py:21
  48.4 0.0 copy-start.5
  48.4 0.0 copy-start.6
  48.5 0.0 copy-start.7
  48.5 146.3 %while.10 = (s32[]{:T(128)}, f32[4,512]{1,0:T(4,128)S(1)}, bf16[4,16,512]{2,1,0:T(8,128)(2,1)S(1)}, s32[4,32,512]{2,0,1:T(4,128)S(1)}, f32[4,32,512]{2,0,1:T(4,1...) while((s32[]{:T(128)}, f32[4,512]{1,0:T(4,128)S(1)}, bf16[4,16,512]{2,1,0:T(8,128)(2,1)S(1)}, ...), condition=%wide.region_3.4_spmd, body=%wide.region_0.3_spmd.sunk | while | flops 451436032 | bytes 13457509 | solution.py:63
  48.5 0.1 constant_dynamic-slice_fusion.4
  48.6 0.1 constant_dynamic-slice_fusion.5
  48.6 30.9 %select_reduce_fusion.3 = f32[3072,512]{1,0:T(8,128)} fusion(f32[32,512]{1,0:T(8,128)S(1)} %bitcast.50, s32[32,512]{1,0:T(8,128)S(1)} %bitcast.51), kind=kLoop, calls=%fused_computation.clone.1 | loop fusion | flops 149422080 | bytes 6422528 | tf_op jit(solution)/shard_map/while/body/eval_jaxpr/reduce_sum | solution.py:31
  79.6 5.4 %fusion.11 = f32[512]{0:T(512)S(1)} fusion(f32[3072,512]{1,0:T(8,128)} %select_reduce_fusion.3, f32[16,3072]{1,0:T(8,128)S(1)} %get-tuple-element.129, bf16[4,16,512]{2,1,0:T(8,128)(2,1)S(1)} %get-tuple-element.126, s32[]{:T(128)} %get-tuple-element.116), kind=kOutput, calls=%fused_computation.4.clone.1 | convolution fusion | flops 302013952 | bytes 6506500 | tf_op jit(solution)/shard_map/while/body/eval_jaxpr/dot_general | solution.py:34
  85.0 0.1 dynamic_update_slice.5
  85.0 0.1 constant_dynamic-slice_fusion.4
  85.1 0.1 constant_dynamic-slice_fusion.5
  85.2 30.9 %select_reduce_fusion.3 = f32[3072,512]{1,0:T(8,128)} fusion(f32[32,512]{1,0:T(8,128)S(1)} %bitcast.50, s32[32,512]{1,0:T(8,128)S(1)} %bitcast.51), kind=kLoop, calls=%fused_computation.clone.1 | loop fusion | flops 149422080 | bytes 6422528 | tf_op jit(solution)/shard_map/while/body/eval_jaxpr/reduce_sum | solution.py:31
  116.1 5.4 %fusion.11 = f32[512]{0:T(512)S(1)} fusion(f32[3072,512]{1,0:T(8,128)} %select_reduce_fusion.3, f32[16,3072]{1,0:T(8,128)S(1)} %get-tuple-element.129, bf16[4,16,512]{2,1,0:T(8,128)(2,1)S(1)} %get-tuple-element.126, s32[]{:T(128)} %get-tuple-element.116), kind=kOutput, calls=%fused_computation.4.clone.1 | convolution fusion | flops 302013952 | bytes 6506500 | tf_op jit(solution)/shard_map/while/body/eval_jaxpr/dot_general | solution.py:34
  121.5 0.1 dynamic_update_slice.5
  121.6 0.1 constant_dynamic-slice_fusion.4
  121.7 0.1 constant_dynamic-slice_fusion.5
  121.8 30.9 %select_reduce_fusion.3 = f32[3072,512]{1,0:T(8,128)} fusion(f32[32,512]{1,0:T(8,128)S(1)} %bitcast.50, s32[32,512]{1,0:T(8,128)S(1)} %bitcast.51), kind=kLoop, calls=%fused_computation.clone.1 | loop fusion | flops 149422080 | bytes 6422528 | tf_op jit(solution)/shard_map/while/body/eval_jaxpr/reduce_sum | solution.py:31
  152.7 5.4 %fusion.11 = f32[512]{0:T(512)S(1)} fusion(f32[3072,512]{1,0:T(8,128)} %select_reduce_fusion.3, f32[16,3072]{1,0:T(8,128)S(1)} %get-tuple-element.129, bf16[4,16,512]{2,1,0:T(8,128)(2,1)S(1)} %get-tuple-element.126, s32[]{:T(128)} %get-tuple-element.116), kind=kOutput, calls=%fused_computation.4.clone.1 | convolution fusion | flops 302013952 | bytes 6506500 | tf_op jit(solution)/shard_map/while/body/eval_jaxpr/dot_general | solution.py:34
  158.1 0.1 dynamic_update_slice.5
  158.2 0.1 constant_dynamic-slice_fusion.4
  158.3 0.1 constant_dynamic-slice_fusion.5
  158.4 30.9 %select_reduce_fusion.3 = f32[3072,512]{1,0:T(8,128)} fusion(f32[32,512]{1,0:T(8,128)S(1)} %bitcast.50, s32[32,512]{1,0:T(8,128)S(1)} %bitcast.51), kind=kLoop, calls=%fused_computation.clone.1 | loop fusion | flops 149422080 | bytes 6422528 | tf_op jit(solution)/shard_map/while/body/eval_jaxpr/reduce_sum | solution.py:31
  189.3 5.4 %fusion.11 = f32[512]{0:T(512)S(1)} fusion(f32[3072,512]{1,0:T(8,128)} %select_reduce_fusion.3, f32[16,3072]{1,0:T(8,128)S(1)} %get-tuple-element.129, bf16[4,16,512]{2,1,0:T(8,128)(2,1)S(1)} %get-tuple-element.126, s32[]{:T(128)} %get-tuple-element.116), kind=kOutput, calls=%fused_computation.4.clone.1 | convolution fusion | flops 302013952 | bytes 6506500 | tf_op jit(solution)/shard_map/while/body/eval_jaxpr/dot_general | solution.py:34
  194.7 0.1 dynamic_update_slice.5
  194.8 5.9 %all-reduce = f32[2048]{0:T(1024)S(1)} all-reduce(f32[2048]{0:T(1024)S(1)} %bitcast.61), channel_id=2, replica_groups=mesh['col'=8,'lev'=4] {'lev'}, use_global_device_ids=true, to_apply=%region_4.5.clone | all-reduce | flops 2048 | bytes 16384
  200.7 0.1 fusion.3
  200.8 0.1 select_reduce_fusion.1
  200.9 5.8 %psum.14 = f32[32]{0:T(128)S(1)} all-reduce(f32[32]{0:T(128)S(1)} %select_reduce_fusion.1), channel_id=1, replica_groups=mesh['col'=8,'lev'=4] {'lev'}, use_global_device_ids=true, to_apply=%region_6.7 | all-reduce | flops 32 | bytes 256 | tf_op jit(solution)/shard_map/psum | solution.py:68
  206.7 20.2 %psum.15 = f32[32]{0:T(128)} all-reduce(f32[32]{0:T(128)S(1)} %psum.14), channel_id=1, replica_groups=mesh['col'=8,'lev'=4] {'col'}, use_global_device_ids=true, to_apply=%region_7.8 | all-reduce | flops 32 | bytes 256 | tf_op jit(solution)/shard_map/psum | solution.py:68
  (23 shorter events, 0.2 us)
Async XLA Ops:
  0.6 8.1 %copy-start.2 = (f32[12,1024]{1,0:T(8,128)S(1)}, f32[12,1024]{1,0:T(8,128)}, u32[]{:S(2)}) copy-start(f32[12,1024]{1,0:T(8,128)} %param.11) | copy-start | bytes 147460
  0.6 42.9 %copy-start = (s32[32,2048]{1,0:T(8,128)S(1)}, s32[32,2048]{1,0:T(8,128)}, u32[]{:S(2)}) copy-start(s32[32,2048]{1,0:T(8,128)} %param.14) | copy-start | bytes 786436
  4.4 39.4 %copy-start.1 = (f32[32,2048]{1,0:T(8,128)S(1)}, f32[32,2048]{1,0:T(8,128)}, u32[]{:S(2)}) copy-start(f32[32,2048]{1,0:T(8,128)} %param.13) | copy-start | bytes 786436
  4.4 39.6 %copy-start.3 = (bf16[16,2048]{1,0:T(8,128)(2,1)S(1)}, bf16[16,2048]{1,0:T(8,128)(2,1)}, u32[]{:S(2)}) copy-start(bf16[16,2048]{1,0:T(8,128)(2,1)} %param.12) | copy-start | bytes 196612
  4.4 39.7 %copy-start.8 = (u32[32]{0:T(128)S(1)}, u32[32]{0:T(128)}, u32[]{:S(2)}) copy-start(u32[32]{0:T(128)} %constant.27) | copy-start | bytes 388
  4.4 32.3 %all-to-all-start = ((bf16[12,64,1024]{2,0,1:T(8,128)(2,1)}), bf16[12,64,1024]{2,0,1:T(8,128)(2,1)S(1)}, u32[]{:S(2)}, u32[]{:S(2)}) async-start(bf16[12,64,1024]{2,0,1:T(8,128)(2,1)} %copy.23), calls=%async_computation | async-start | bytes 4194304 | tf_op jit(solution)/shard_map/all_to_all | solution.py:42
  38.0 7.3 %collective-permute-start = (f32[16,1024]{1,0:T(8,128)S(1)}, f32[16,1024]{1,0:T(8,128)S(1)}, u32[]{:S(2)}, u32[]{:S(2)}) collective-permute-start(f32[16,1024]{1,0:T(8,128)S(1)} %bitcast.55), channel_id=1, source_target_pairs={{0,4},{4,8},{8,12},{12,16},{16,20},{20,24},{24,28},{1,5},{5,9},{9,... | collective-permute-start | bytes 196616 | tf_op jit(solution)/shard_map/ppermute | solution.py:19
  42.3 6.2 %collective-permute-start.1 = (f32[16,1024]{1,0:T(8,128)S(1)}, f32[16,1024]{1,0:T(8,128)S(1)}, u32[]{:S(2)}, u32[]{:S(2)}) collective-permute-start(f32[16,1024]{1,0:T(8,128)S(1)} %bitcast.56), channel_id=1, source_target_pairs={{4,0},{8,4},{12,8},{16,12},{20,16},{24,20},{28,24},{5,1},{9,5},{13... | collective-permute-start | bytes 196616 | tf_op jit(solution)/shard_map/ppermute | solution.py:21
  48.4 152.2 %copy-start.5 = (f32[512]{0:T(512)S(1)}, f32[512]{0:T(512)}, u32[]{:S(2)}) copy-start(f32[512]{0:T(512)} %param.15) | copy-start | bytes 6148
  48.4 152.2 %copy-start.6 = (s32[512]{0:T(512)S(1)}, s32[512]{0:T(512)}, u32[]{:S(2)}) copy-start(s32[512]{0:T(512)} %param.17) | copy-start | bytes 6148
  48.5 152.3 %copy-start.7 = (s32[512]{0:T(512)S(1)}, s32[512]{0:T(512)}, u32[]{:S(2)}) copy-start(s32[512]{0:T(512)} %param.16) | copy-start | bytes 6148
  200.7 26.2 %copy-start.4 = (f32[512]{0:T(512)}, f32[512]{0:T(512)S(1)}, u32[]{:S(2)}) copy-start(f32[512]{0:T(512)S(1)} %fusion.3) | copy-start | bytes 6148
